TPU v7x, 32 devices: a whole 2x2x4 slice. The times are simulated.
32 devices in a mesh: groups: 2 (over y), ctx: 4 (over z), mp: 4 (over x, core).
Axes of the slice: x: 2, y: 2, z: 4, core: 2. Of those that a mesh axis runs over, the one named last changes fastest.
Arguments:
- streams: bfloat16 [3, 2048, 4096], P(None, ('groups', 'ctx'), 'mp'), parts along dimension 1, may hold values from -6 to 6
- short_filter: float32 [3, 3, 4096], P(None, None, 'mp'), may hold values from -3 to 3
- mode_params: float32 [2, 4096, 8], P(None, 'mp'), may hold values from -2 to 2, as said below
- out_weight: bfloat16 [4096, 4096], P('mp', 'ctx'), may hold values from -0.09375 to 0.09375
- norm_gain: float32 [4096], P('mp'), may hold values from 0.5 to 1.5
- unembed: bfloat16 [4096, 512], P('mp'), may hold values from -40 to 40
- native: int32 [2048], P(('groups', 'ctx')), parts along dimension 0, may hold values from 0 to 511
- mut_pos: int32 [512], P('groups'), parts along dimension 0, may hold values from 0 to 1023
- mut_ids: int32 [512], P('groups'), parts along dimension 0, may hold values from 0 to 511
Outputs:
- loglik: float32 [2048], P(('groups', 'ctx')), parts along dimension 0
- scores: float32 [512], P('groups'), parts along dimension 0
There are 2 independent parts, one for each index of `groups`. A program takes and returns all parts, laid end to end along the dimension named above; an argument that names none is the same for every part. Nothing has to cross between parts.
Inputs may be any that keep to these rules, and one draw needn't show every extreme that they name: mode_params[0] holds positive decay rates, mode_params[1] residues.
All inputs are finite; a program needn't handle non-finite values.
Results may differ from a plain program's by a relative error of at most 0.0065.
Values may be sent and summed in bfloat16 or wider, within the bound.
No kernel may reach another device: no remote copies, remote signals or barrier semaphores. Data moves between devices by JAX's collectives and lax.ppermute only.
A program may use at most 192 MiB of HBM per device.

v0:
```python
import jax
import jax.numpy as jnp
from jax import lax
from jax.sharding import PartitionSpec as P

D = 4096
PRECISE = lax.Precision.HIGHEST


def from_behind(value, axis, steps):
    count = lax.axis_size(axis)
    initial, last = (max(0, -steps), min(count, count - steps))
    return lax.ppermute(value, axis, [(source, source + steps) for source in range(initial, last)])


def prefix(value, axis, join, neutral):
    count, mine = (lax.axis_size(axis), lax.axis_index(axis))
    pieces = jax.tree.map(lambda part: lax.all_gather(part, axis), value)
    so_far = jax.tree.map(
        lambda part, zero: jnp.full_like(part, 0) + jnp.asarray(zero, part.dtype), value, neutral
    )

    def hop(position, so_far):
        longer = join(so_far, jax.tree.map(lambda part: part[position], pieces))
        return jax.tree.map(lambda new, old: jnp.where(position < mine, new, old), longer, so_far)

    return lax.fori_loop(0, count - 1, hop, so_far)


def short_mix(padded, short_filter, seq_rows):
    return (
        short_filter[:, 0, None, :] * padded[:, 2:, :]
        + short_filter[:, 1, None, :] * padded[:, 1 : seq_rows + 1, :]
        + short_filter[:, 2, None, :] * padded[:, 0:seq_rows, :]
    )


def carry_terms(starts, decays, residue, span_len):
    lag_steps = jnp.arange(span_len, dtype=jnp.float32)
    weights = residue[None] * jnp.exp(-decays[None] * (lag_steps + 1.0)[:, None, None])
    return jnp.einsum("ncm,tcm->ntc", starts, weights, precision=PRECISE)


def span_conv(values, decays, residue, span_len):
    seq_all, channels = values.shape
    spans = seq_all // span_len
    lag_steps = jnp.arange(span_len, dtype=jnp.float32)
    powers = jnp.exp(-decays[None] * lag_steps[:, None, None])
    kernel = jnp.sum(residue[None] * powers, axis=2)
    offsets = jnp.arange(span_len, dtype=jnp.int32)
    spread = offsets[:, None] - offsets[None, :]
    toeplitz = jnp.where((spread >= 0)[:, :, None], kernel[jnp.clip(spread, 0, span_len - 1)], 0.0)
    blocked = values.reshape(spans, span_len, channels)
    inside = jnp.einsum("tsc,nsc->ntc", toeplitz, blocked, precision=PRECISE)
    tail_pows = jnp.exp(-decays[None] * (span_len - 1.0 - lag_steps)[:, None, None])
    own_states = jnp.einsum("nsc,scm->ncm", blocked, tail_pows, precision=PRECISE)
    factor = jnp.exp(-decays * span_len)

    def advance(carried, own_part):
        return (factor * carried + own_part, carried)

    end_state, starts = lax.scan(advance, jnp.zeros_like(factor), own_states)
    result = inside + carry_terms(starts, decays, residue, span_len)
    return (result.reshape(seq_all, channels), end_state)


def enter_terms(entering, decays, residue, spans, span_len):
    span_index = jnp.arange(spans, dtype=jnp.float32)
    starts = jnp.exp(-decays[None] * (span_index * span_len)[:, None, None]) * entering[None]
    added = carry_terms(starts, decays, residue, span_len)
    return added.reshape(spans * span_len, decays.shape[0])


def chain_pair(earlier, following):
    return (earlier[0] * following[0], following[0] * earlier[1] + following[1])


def body(
    streams, short_filter, mode_params, out_weight, norm_gain, unembed, native, mut_pos, mut_ids
):
    seq_rows = streams.shape[1]
    prior = from_behind(streams[:, seq_rows - 2 :, :], "ctx", 1)
    padded = jnp.concatenate([prior, streams], axis=1).astype(jnp.float32)
    mixed = short_mix(padded, short_filter, seq_rows)
    gate_bf = lax.optimization_barrier(mixed[0].astype(jnp.bfloat16))
    product = (mixed[1] * mixed[2]).astype(jnp.bfloat16)
    decays = mode_params[0]
    residue = mode_params[1]
    span_len = min(64, seq_rows)
    spans = seq_rows // span_len
    inside, own_end = span_conv(product.astype(jnp.float32), decays, residue, span_len)
    factor = jnp.exp(-decays * seq_rows)
    unused, entering = prefix(
        (factor, own_end), "ctx", chain_pair, (jnp.ones_like(factor), jnp.zeros_like(own_end))
    )
    conv_sum = inside + enter_terms(entering, decays, residue, spans, span_len)
    conv_bf = conv_sum.astype(jnp.bfloat16)
    conv_bf = lax.optimization_barrier(conv_bf)
    gated = (gate_bf.astype(jnp.float32) * conv_bf.astype(jnp.float32)).astype(jnp.bfloat16)
    terms = jnp.dot(
        gated,
        lax.all_gather(out_weight, "ctx", axis=1, tiled=True),
        preferred_element_type=jnp.float32,
    )
    output = lax.psum_scatter(terms, "mp", scatter_dimension=1, tiled=True)
    squares = lax.psum(jnp.sum(output * output, axis=1), "mp")
    normed = (output * lax.rsqrt(squares[:, None] / D + 1e-05) * norm_gain).astype(jnp.bfloat16)
    logit_terms = jnp.dot(normed, unembed, preferred_element_type=jnp.float32)
    local_pos = mut_pos - lax.axis_index("ctx") * seq_rows
    owned_mut = (local_pos >= 0) & (local_pos < seq_rows)
    slot_rows = jnp.clip(local_pos, 0, seq_rows - 1)
    logits = lax.psum(logit_terms, "mp")
    vocab_ids = jnp.arange(logits.shape[1], dtype=jnp.int32)
    totals = jax.nn.logsumexp(logits, axis=1)
    picked = jnp.sum(jnp.where(vocab_ids[None, :] == native[:, None], logits, 0.0), axis=1)
    chosen = jnp.sum(
        jnp.where(vocab_ids[None, :] == mut_ids[:, None], logits[slot_rows], 0.0), axis=1
    )
    loglik = picked - totals
    mut_terms = jnp.where(owned_mut, chosen - picked[slot_rows], 0.0)
    scores = lax.psum(mut_terms, "ctx")
    return (loglik, scores)


def solution(mesh):
    in_specs = (
        P(None, ("groups", "ctx"), "mp"),
        P(None, None, "mp"),
        P(None, "mp", None),
        P("mp", "ctx"),
        P("mp"),
        P("mp", None),
        P(("groups", "ctx")),
        P("groups"),
        P("groups"),
    )
    out_specs = (P(("groups", "ctx")), P("groups"))
    return jax.shard_map(body, mesh=mesh, in_specs=in_specs, out_specs=out_specs, check_vma=False)
```

profile of v0, /device:TPU:0, one launch (start us, length us, event | category | flops | bytes accessed | tf_op | source)
XLA Modules:
  0.0 301.2 jit_solution(9533523569857050880)
XLA Ops:
  8.0 0.8 slice.38
  8.8 5.0 %collective-permute-start = (bf16[3,2,1024]{2,1,0:T(2,128)(2,1)S(1)}, bf16[3,2,1024]{2,1,0:T(2,128)(2,1)S(1)}, u32[]{:S(2)}, u32[]{:S(2)}) collective-permute-start(bf16[3,2,1024]{2,1,0:T(2,128)(2,1)S(1)} %slice.38), channel_id=1, source_target_pairs={{0,4},{4,8},{8,12},{1,5},{5,9},{9,13},{2,6},{6,10},{10,14},{3,7},{... | collective-permute-start | bytes 36872 | tf_op jit(solution)/shard_map/ppermute | solution.py:13
  13.8 0.8 exponential_bitcast_fusion
  15.2 5.8 %multiply_reduce_fusion = f32[64,1024]{0,1:T(8,128)S(1)} fusion(f32[1024,8]{1,0:T(8,128)S(1)} %copy.32, f32[1024,8]{1,0:T(8,128)S(1)} %copy.31), kind=kLoop, calls=%fused_computation.18 | loop fusion | flops 1507328 | bytes 327680 | tf_op jit(solution)/shard_map/reduce_sum | solution.py:49
  21.0 20.9 %all_gather.13 = f32[4,1024,8]{1,2,0:T(8,128)S(1)} all-gather(f32[1,1024,8]{1,2,0:T(8,128)S(1)} %get-tuple-element.201), channel_id=1, replica_groups=mesh['groups'=2,'ctx'=4,'mp'=4] {'ctx'}, dimensions={0}, use_global_device_ids=true | all-gather | bytes 163840 | tf_op jit(solution)/shard_map/all_gather | solution.py:18
  42.1 18.4 %gather_fusion = f32[4096,1024]{1,0:T(8,128)} fusion(f32[64,1024]{1,0:T(8,128)S(1)} %copy.33, s32[4096]{0:T(1024)S(1)} %broadcast_clamp_fusion), kind=kCustom, calls=%fused_computation | custom fusion | bytes 33570816 | tf_op jit(solution)/shard_map/gather | solution.py:52
  60.6 30.5 %copy.34 = f32[64,64,1024]{1,0,2:T(8,128)} copy(f32[64,64,1024]{2,1,0:T(8,128)} %bitcast.58) | data formatting | bytes 33554432 | tf_op jit(solution)/shard_map/gather | solution.py:52
  91.1 1.9 maximum_convert_fusion
  93.0 0.9 fusion.10
  93.9 1.6 copy-done.2
  95.7 0.7 copy.35
  96.4 6.0 %fusion.26 = f32[4,1024,8]{2,0,1:T(4,128)} fusion(bf16[4,64,1024]{1,0,2:T(4,128)(2,1)S(1)} %copy.35, f32[64]{0:T(128)S(1)} %iota_subtract_fusion, f32[1024,8]{1,0:T(8,128)S(1)} %copy.32), kind=kOutput, calls=%fused_computation.38 | convolution fusion | flops 25690112 | bytes 688384 | tf_op jit(solution)/shard_map/nsc,scm->ncm/dot_general | solution.py:56
  102.4 1.9 copy.37
  104.3 2.5 while.27
  106.9 15.5 %all-gather = f32[4096,8]{0,1:T(8,128)S(1)} all-gather(f32[1024,8]{0,1:T(8,128)S(1)} %get-tuple-element.125), channel_id=2, replica_groups=mesh['groups'=2,'ctx'=4,'mp'=4] {'ctx'}, dimensions={0}, use_global_device_ids=true | all-gather | bytes 163840 | tf_op jit(solution)/shard_map/all_gather | solution.py:18
  122.5 1.0 copy.40
  123.5 2.5 copy.38
  126.0 10.4 %fusion.8 = f32[1024,64,4]{1,2,0:T(4,128)S(1)} fusion(f32[64]{0:T(128)S(1)} %iota_add_fusion, f32[1024,8]{1,0:T(8,128)S(1)} %copy.32, f32[1024,8]{1,0:T(8,128)S(1)} %copy-done.4, f32[1024,8]{1,0:T(8,128)} %copy.40, f32[4]{0:T(128)S(1)} %iota_multiply_fusion), kind=kOutput, calls=%fused_computation.16 | convolution fusion | flops 26279936 | bytes 1147152 | tf_op jit(solution)/shard_map/ncm,tcm->ntc/dot_general | solution.py:41
  136.5 9.8 %fusion.9 = f32[1024,64,4]{1,2,0:T(4,128)S(1)} fusion(f32[4,1024,8]{2,0,1:T(4,128)S(1)} %copy-done.5, f32[64]{0:T(128)S(1)} %iota_add_fusion, f32[1024,8]{1,0:T(8,128)S(1)} %copy.32, f32[1024,8]{1,0:T(8,128)S(1)} %copy-done.4), kind=kOutput, calls=%fused_computation.17 | convolution fusion | flops 26214400 | bytes 1245440 | tf_op jit(solution)/shard_map/ncm,tcm->ntc/dot_general | solution.py:41
  146.2 29.9 %fusion.12 = bf16[4,64,1024]{1,0,2:T(4,128)(2,1)S(1)} fusion(f32[1024,64,4]{1,2,0:T(4,128)S(1)} %fusion.8, f32[1024,64,4]{1,2,0:T(4,128)S(1)} %fusion.9, bf16[4,64,1024]{1,0,2:T(4,128)(2,1)S(1)} %copy.35, f32[64,64,1024]{1,0,2:T(8,128)} %copy.34, pred[64,64]{1,0:T(8,128)(4,1)S(1)} %subtract_compare_fusion), kind=kOutput, calls=%fused_computation.25 | convolution fusion | flops 206307328 | bytes 19927040 | tf_op jit(solution)/shard_map/tsc,nsc->ntc/dot_general | solution.py:54
  176.8 1.3 fusion.35
  178.1 7.6 %fusion.33 = f32[256,4096]{1,0:T(8,128)} fusion(bf16[1024,4096]{1,0:T(8,128)(2,1)} %all-gather.3.cloned.1.call-done, bf16[256,1024]{1,0:T(8,128)(2,1)S(1)} %bitcast.59, bf16[256,1024]{1,0:T(8,128)(2,1)S(1)} %fusion.35), kind=kOutput, calls=%fused_computation.49 | convolution fusion | flops 2148532224 | bytes 13631488 | tf_op jit(solution)/shard_map/dot_general | solution.py:100
  185.8 46.4 %reduce-scatter.2.cloned.1.call-done = f32[256,1024]{1,0:T(8,128)} async-done(((f32[256,4096]{1,0:T(8,128)}), f32[256,1024]{1,0:T(8,128)}) %reduce-scatter.2.cloned.1.call-update) | async-done | bytes 1048592 | tf_op jit(solution)/shard_map/reduce_scatter | solution.py:105
  232.2 1.4 multiply_reduce_fusion.1
  233.6 5.8 %psum.21 = f32[256]{0:T(256)S(1)} all-reduce(f32[256]{0:T(256)S(1)} %multiply_reduce_fusion.1), channel_id=1, replica_groups=mesh['groups'=2,'ctx'=4,'mp'=4] {'mp'}, use_global_device_ids=true, to_apply=%region_7.8 | all-reduce | flops 256 | bytes 2048 | tf_op jit(solution)/shard_map/psum | solution.py:106
  239.4 2.5 fusion.34
  242.0 34.1 %all-reduce.2.cloned.1.call-done = f32[256,512]{1,0:T(8,128)} async-done(((f32[256,512]{1,0:T(8,128)}), f32[256,512]{1,0:T(8,128)}) %all-reduce.2.cloned.1.call-update) | async-done | bytes 524304 | tf_op jit(solution)/shard_map/psum | solution.py:112
  276.1 1.2 reduce_max.9
  277.4 1.3 exponential_reduce_fusion
  278.7 1.9 gather_fusion.2
  280.7 1.0 gather_fusion.1
  281.9 12.2 %psum.23 = f32[256]{0:T(256)} all-reduce(f32[256]{0:T(256)S(1)} %and_select_fusion), channel_id=1, replica_groups=mesh['groups'=2,'ctx'=4,'mp'=4] {'ctx'}, use_global_device_ids=true, to_apply=%region_13.14 | all-reduce | flops 256 | bytes 2048 | tf_op jit(solution)/shard_map/psum | solution.py:121
  (66 shorter events, 5.8 us)
Async XLA Ops:
  7.2 232.2 %copy-start = (bf16[1024,512]{1,0:T(8,128)(2,1)S(1)}, bf16[1024,512]{1,0:T(8,128)(2,1)}, u32[]{:S(2)}) copy-start(bf16[1024,512]{1,0:T(8,128)(2,1)} %param.18) | copy-start | bytes 3145732
  7.2 7.9 %copy-start.6 = (f32[3,3,1024]{2,1,0:T(4,128)S(1)}, f32[3,3,1024]{2,1,0:T(4,128)}, u32[]{:S(2)}) copy-start(f32[3,3,1024]{2,1,0:T(4,128)} %param.14) | copy-start | bytes 110596
  7.2 170.9 %all-gather.3.cloned.1.call-start = ((), (), s32[]{:S(2)}) async-start(), calls=%async_computation.1 | async-start | bytes 10485760 | tf_op jit(solution)/shard_map/all_gather | solution.py:102
  7.9 224.3 %reduce-scatter.2.cloned.1.call-start = ((), (), s32[]{:S(2)}) async-start(), calls=%async_computation.2 | async-start | bytes 5242880 | tf_op jit(solution)/shard_map/reduce_scatter | solution.py:105
  8.8 82.3 %collective-permute-start = (bf16[3,2,1024]{2,1,0:T(2,128)(2,1)S(1)}, bf16[3,2,1024]{2,1,0:T(2,128)(2,1)S(1)}, u32[]{:S(2)}, u32[]{:S(2)}) collective-permute-start(bf16[3,2,1024]{2,1,0:T(2,128)(2,1)S(1)} %slice.38), channel_id=1, source_target_pairs={{0,4},{4,8},{8,12},{1,5},{5,9},{9,13},{2,6},{6,10},{10,14},{3,7},{... | collective-permute-start | bytes 36872 | tf_op jit(solution)/shard_map/ppermute | solution.py:13
  15.0 27.0 %copy-start.3 = (f32[1024,8]{1,0:T(8,128)}, f32[1024,8]{1,0:T(8,128)S(1)}, u32[]{:S(2)}) copy-start(f32[1024,8]{1,0:T(8,128)S(1)} %copy.31) | copy-start | bytes 98308
  93.9 1.6 copy-start.2
  102.4 23.6 %copy-start.4 = (f32[1024,8]{1,0:T(8,128)S(1)}, f32[1024,8]{1,0:T(8,128)}, u32[]{:S(2)}) copy-start(f32[1024,8]{1,0:T(8,128)} %copy-done.3) | copy-start | bytes 98308
  126.0 10.4 %copy-start.5 = (f32[4,1024,8]{2,0,1:T(4,128)S(1)}, f32[4,1024,8]{2,0,1:T(4,128)}, u32[]{:S(2)}) copy-start(f32[4,1024,8]{2,0,1:T(4,128)} %copy.38) | copy-start | bytes 393220
  185.7 53.7 %copy-start.7 = (f32[1024]{0:T(1024)S(1)}, f32[1024]{0:T(1024)}, u32[]{:S(2)}) copy-start(f32[1024]{0:T(1024)} %param.17) | copy-start | bytes 12292
  185.7 56.2 %copy-start.8 = (s32[256]{0:T(256)S(1)}, s32[256]{0:T(256)}, u32[]{:S(2)}) copy-start(s32[256]{0:T(256)} %param.20) | copy-start | bytes 3076
  185.8 91.6 %copy-start.9 = (s32[256]{0:T(256)S(1)}, s32[256]{0:T(256)}, u32[]{:S(2)}) copy-start(s32[256]{0:T(256)} %param.19) | copy-start | bytes 3076
  185.8 90.3 %all-reduce.2.cloned.1.call-start = ((), (), s32[]{:S(2)}) async-start(), calls=%async_computation.3 | async-start | bytes 1048576 | tf_op jit(solution)/shard_map/psum | solution.py:112
  276.1 4.6 %copy-start.1 = (f32[256,512]{1,0:T(8,128)S(1)}, f32[256,512]{1,0:T(8,128)}, u32[]{:S(2)}) copy-start(f32[256,512]{1,0:T(8,128)} %all-reduce.2.cloned.1.call-done) | copy-start | bytes 1572868
  277.4 4.3 %copy-start.10 = (s32[256]{0:T(256)S(1)}, s32[256]{0:T(256)}, u32[]{:S(2)}) copy-start(s32[256]{0:T(256)} %param.21) | copy-start | bytes 3076
Sparse Core Ops, SparseCore 0:
  9.6 156.0 all-gather.2
  185.9 46.3 reduce-scatter.1
  242.0 34.0 all-reduce.1
where the time goes:
time: 303 us; the launch traced here: 301 us
  waiting for transfers between devices  81.3 us (27%)
  matrix products  66.2 us (22%)
  local copies, waits for them, and re-layouts  63.1 us (21%)
  blocking collectives  54.4 us (18%)
  other arithmetic  16.9 us (6%)
  between operations  14.1 us (5%)
  starting transfers between devices  5.07 us (2%)
    gather x2, local copies, waits for them, and re-layouts, span_conv(): kernel[jnp.clip(spread, 0, span_len - 1)]  48.9 us
    reduce_scatter x1, waiting for transfers between devices, body(): output = lax.psum_scatter(terms, 'mp', scatter_dimension=1, tiled=True)  46.4 us
    all_gather x2, blocking collectives, prefix(): pieces = jax.tree.map(lambda part: lax.all_gather(part, axis), value)  36.4 us
    psum x1, waiting for transfers between devices, body(): logits = lax.psum(logit_terms, 'mp')  34.1 us
    dot_general x1, matrix products, span_conv(): inside = jnp.einsum('tsc,nsc->ntc', toeplitz, blocked, precision=PRECISE)  29.9 us
    dot_general x2, matrix products, carry_terms(): return jnp.einsum('ncm,tcm->ntc', starts, weights, precision=PRECISE)  20.2 us
    psum x1, blocking collectives, body(): scores = lax.psum(mut_terms, 'ctx')  12.2 us
    dot_general x1, matrix products, body(): jnp.dot(gated, lax.all_gather(out_weight, 'ctx', axis=1, tiled=True), pre...  7.64 us
  transfers between devices with their start and end apart: 4, of which 2 were waited for; matrix products, arithmetic and copies ran while one was open for 42% of the time, Pallas kernels for 0%

commit v1 on v0

--- a/solution.py
+++ b/solution.py
@@ -109,7 +109,7 @@
     local_pos = mut_pos - lax.axis_index("ctx") * seq_rows
     owned_mut = (local_pos >= 0) & (local_pos < seq_rows)
     slot_rows = jnp.clip(local_pos, 0, seq_rows - 1)
-    logits = lax.psum(logit_terms, "mp")
+    logits = lax.all_gather(logit_terms, "mp").sum(axis=0)
     vocab_ids = jnp.arange(logits.shape[1], dtype=jnp.int32)
     totals = jax.nn.logsumexp(logits, axis=1)
     picked = jnp.sum(jnp.where(vocab_ids[None, :] == native[:, None], logits, 0.0), axis=1)

time: 303 us -> 291 us (0.960)
  waiting for transfers between devices: 81.3 us -> 70.5 us
    psum x1 -> x0, waiting for transfers between devices: 34.1 us -> none  [body(): logits = lax.psum(logit_terms, 'mp')]
    all_gather x0 -> x1, waiting for transfers between devices: none -> 23.3 us  [body(): logits = lax.all_gather(logit_terms, 'mp').sum(axis=0)]
  transfers between devices with their start and end apart: 4 -> 4, of which waited for: 2 -> 2; matrix products, arithmetic and copies ran while one was open for 42% -> 44% of each run, Pallas kernels for 0% -> 0%
where the time goes in v1:
time: 291 us; the launch traced here: 290 us
  waiting for transfers between devices  70.5 us (24%)
  matrix products  66.2 us (23%)
  local copies, waits for them, and re-layouts  63.1 us (22%)
  blocking collectives  54.4 us (19%)
  other arithmetic  16.6 us (6%)
  between operations  14.1 us (5%)
  starting transfers between devices  5.07 us (2%)
    gather x2, local copies, waits for them, and re-layouts, span_conv(): kernel[jnp.clip(spread, 0, span_len - 1)]  48.9 us
    reduce_scatter x1, waiting for transfers between devices, body(): output = lax.psum_scatter(terms, 'mp', scatter_dimension=1, tiled=True)  46.4 us
    all_gather x2, blocking collectives, prefix(): pieces = jax.tree.map(lambda part: lax.all_gather(part, axis), value)  36.4 us
    dot_general x1, matrix products, span_conv(): inside = jnp.einsum('tsc,nsc->ntc', toeplitz, blocked, precision=PRECISE)  29.9 us
    all_gather x1, waiting for transfers between devices, body(): logits = lax.all_gather(logit_terms, 'mp').sum(axis=0)  23.3 us
    dot_general x2, matrix products, carry_terms(): return jnp.einsum('ncm,tcm->ntc', starts, weights, precision=PRECISE)  20.2 us
    psum x1, blocking collectives, body(): scores = lax.psum(mut_terms, 'ctx')  12.2 us
    dot_general x1, matrix products, body(): jnp.dot(gated, lax.all_gather(out_weight, 'ctx', axis=1, tiled=True), pre...  7.64 us
  transfers between devices with their start and end apart: 4, of which 2 were waited for; matrix products, arithmetic and copies ran while one was open for 44% of the time, Pallas kernels for 0%

profile of v1, /device:TPU:0, one launch (start us, length us, event | category | flops | bytes accessed | tf_op | source)
XLA Modules:
  0.0 290.1 jit_solution(14660191212644134595)
XLA Ops:
  7.2 0.7 all-gather.5.cloned.1.call-update
  8.0 0.8 slice.38
  8.8 5.0 %collective-permute-start = (bf16[3,2,1024]{2,1,0:T(2,128)(2,1)S(1)}, bf16[3,2,1024]{2,1,0:T(2,128)(2,1)S(1)}, u32[]{:S(2)}, u32[]{:S(2)}) collective-permute-start(bf16[3,2,1024]{2,1,0:T(2,128)(2,1)S(1)} %slice.38), channel_id=1, source_target_pairs={{0,4},{4,8},{8,12},{1,5},{5,9},{9,13},{2,6},{6,10},{10,14},{3,7},{... | collective-permute-start | bytes 36872 | tf_op jit(solution)/shard_map/ppermute | solution.py:13
  13.8 0.8 exponential_bitcast_fusion
  15.2 5.8 %multiply_reduce_fusion = f32[64,1024]{0,1:T(8,128)S(1)} fusion(f32[1024,8]{1,0:T(8,128)S(1)} %copy.32, f32[1024,8]{1,0:T(8,128)S(1)} %copy.31), kind=kLoop, calls=%fused_computation.18 | loop fusion | flops 1507328 | bytes 327680 | tf_op jit(solution)/shard_map/reduce_sum | solution.py:49
  21.0 20.9 %all_gather.19 = f32[4,1024,8]{1,2,0:T(8,128)S(1)} all-gather(f32[1,1024,8]{1,2,0:T(8,128)S(1)} %get-tuple-element.201), channel_id=1, replica_groups=mesh['groups'=2,'ctx'=4,'mp'=4] {'ctx'}, dimensions={0}, use_global_device_ids=true | all-gather | bytes 163840 | tf_op jit(solution)/shard_map/all_gather | solution.py:18
  42.1 18.4 %gather_fusion = f32[4096,1024]{1,0:T(8,128)} fusion(f32[64,1024]{1,0:T(8,128)S(1)} %copy.33, s32[4096]{0:T(1024)S(1)} %broadcast_clamp_fusion), kind=kCustom, calls=%fused_computation | custom fusion | bytes 33570816 | tf_op jit(solution)/shard_map/gather | solution.py:52
  60.6 30.5 %copy.34 = f32[64,64,1024]{1,0,2:T(8,128)} copy(f32[64,64,1024]{2,1,0:T(8,128)} %bitcast.59) | data formatting | bytes 33554432 | tf_op jit(solution)/shard_map/gather | solution.py:52
  91.1 1.9 maximum_convert_fusion
  93.0 0.9 fusion.10
  93.9 1.6 copy-done.1
  95.7 0.7 copy.35
  96.4 6.0 %fusion.26 = f32[4,1024,8]{2,0,1:T(4,128)} fusion(bf16[4,64,1024]{1,0,2:T(4,128)(2,1)S(1)} %copy.35, f32[64]{0:T(128)S(1)} %iota_subtract_fusion, f32[1024,8]{1,0:T(8,128)S(1)} %copy.32), kind=kOutput, calls=%fused_computation.38 | convolution fusion | flops 25690112 | bytes 688384 | tf_op jit(solution)/shard_map/nsc,scm->ncm/dot_general | solution.py:56
  102.4 1.9 copy.37
  104.3 2.5 while.27
  106.9 15.5 %all-gather = f32[4096,8]{0,1:T(8,128)S(1)} all-gather(f32[1024,8]{0,1:T(8,128)S(1)} %get-tuple-element.125), channel_id=2, replica_groups=mesh['groups'=2,'ctx'=4,'mp'=4] {'ctx'}, dimensions={0}, use_global_device_ids=true | all-gather | bytes 163840 | tf_op jit(solution)/shard_map/all_gather | solution.py:18
  122.5 1.0 copy.40
  123.5 2.5 copy.38
  126.0 10.4 %fusion.8 = f32[1024,64,4]{1,2,0:T(4,128)S(1)} fusion(f32[64]{0:T(128)S(1)} %iota_add_fusion, f32[1024,8]{1,0:T(8,128)S(1)} %copy.32, f32[1024,8]{1,0:T(8,128)S(1)} %copy-done.3, f32[1024,8]{1,0:T(8,128)} %copy.40, f32[4]{0:T(128)S(1)} %iota_multiply_fusion), kind=kOutput, calls=%fused_computation.16 | convolution fusion | flops 26279936 | bytes 1147152 | tf_op jit(solution)/shard_map/ncm,tcm->ntc/dot_general | solution.py:41
  136.5 9.8 %fusion.9 = f32[1024,64,4]{1,2,0:T(4,128)S(1)} fusion(f32[4,1024,8]{2,0,1:T(4,128)S(1)} %copy-done.4, f32[64]{0:T(128)S(1)} %iota_add_fusion, f32[1024,8]{1,0:T(8,128)S(1)} %copy.32, f32[1024,8]{1,0:T(8,128)S(1)} %copy-done.3), kind=kOutput, calls=%fused_computation.17 | convolution fusion | flops 26214400 | bytes 1245440 | tf_op jit(solution)/shard_map/ncm,tcm->ntc/dot_general | solution.py:41
  146.2 29.9 %fusion.12 = bf16[4,64,1024]{1,0,2:T(4,128)(2,1)S(1)} fusion(f32[1024,64,4]{1,2,0:T(4,128)S(1)} %fusion.8, f32[1024,64,4]{1,2,0:T(4,128)S(1)} %fusion.9, bf16[4,64,1024]{1,0,2:T(4,128)(2,1)S(1)} %copy.35, f32[64,64,1024]{1,0,2:T(8,128)} %copy.34, pred[64,64]{1,0:T(8,128)(4,1)S(1)} %subtract_compare_fusion), kind=kOutput, calls=%fused_computation.25 | convolution fusion | flops 206307328 | bytes 19927040 | tf_op jit(solution)/shard_map/tsc,nsc->ntc/dot_general | solution.py:54
  176.8 1.3 fusion.35
  178.1 7.6 %fusion.33 = f32[256,4096]{1,0:T(8,128)} fusion(bf16[1024,4096]{1,0:T(8,128)(2,1)} %all-gather.5.cloned.1.call-done, bf16[256,1024]{1,0:T(8,128)(2,1)S(1)} %bitcast.60, bf16[256,1024]{1,0:T(8,128)(2,1)S(1)} %fusion.35), kind=kOutput, calls=%fused_computation.49 | convolution fusion | flops 2148532224 | bytes 13631488 | tf_op jit(solution)/shard_map/dot_general | solution.py:100
  185.8 46.4 %reduce-scatter.2.cloned.1.call-done = f32[256,1024]{1,0:T(8,128)} async-done(((f32[256,4096]{1,0:T(8,128)}), f32[256,1024]{1,0:T(8,128)}) %reduce-scatter.2.cloned.1.call-update) | async-done | bytes 1048592 | tf_op jit(solution)/shard_map/reduce_scatter | solution.py:105
  232.2 1.4 multiply_reduce_fusion.1
  233.6 5.8 %psum.14 = f32[256]{0:T(256)S(1)} all-reduce(f32[256]{0:T(256)S(1)} %multiply_reduce_fusion.1), channel_id=1, replica_groups=mesh['groups'=2,'ctx'=4,'mp'=4] {'mp'}, use_global_device_ids=true, to_apply=%region_7.8 | all-reduce | flops 256 | bytes 2048 | tf_op jit(solution)/shard_map/psum | solution.py:106
  239.4 2.5 fusion.34
  242.0 23.3 %all-gather.7.cloned.1.call-done = f32[1024,512]{1,0:T(8,128)} async-done(((f32[256,512]{1,0:T(8,128)}), f32[1024,512]{1,0:T(8,128)}) %all-gather.7.cloned.1.call-update) | async-done | bytes 2097168 | tf_op jit(solution)/shard_map/all_gather | solution.py:112
  265.3 1.9 reduce_sum.56
  267.2 1.0 gather_fusion.1
  268.6 1.9 gather_fusion.2
  270.8 12.2 %psum.15 = f32[256]{0:T(256)} all-reduce(f32[256]{0:T(256)S(1)} %and_select_fusion), channel_id=1, replica_groups=mesh['groups'=2,'ctx'=4,'mp'=4] {'ctx'}, use_global_device_ids=true, to_apply=%region_13.14 | all-reduce | flops 256 | bytes 2048 | tf_op jit(solution)/shard_map/psum | solution.py:121
  (65 shorter events, 5.6 us)
Async XLA Ops:
  7.2 232.2 %copy-start = (bf16[1024,512]{1,0:T(8,128)(2,1)S(1)}, bf16[1024,512]{1,0:T(8,128)(2,1)}, u32[]{:S(2)}) copy-start(bf16[1024,512]{1,0:T(8,128)(2,1)} %param.18) | copy-start | bytes 3145732
  7.2 7.9 %copy-start.5 = (f32[3,3,1024]{2,1,0:T(4,128)S(1)}, f32[3,3,1024]{2,1,0:T(4,128)}, u32[]{:S(2)}) copy-start(f32[3,3,1024]{2,1,0:T(4,128)} %param.14) | copy-start | bytes 110596
  7.2 170.9 %all-gather.5.cloned.1.call-start = ((), (), s32[]{:S(2)}) async-start(), calls=%async_computation.1 | async-start | bytes 10485760 | tf_op jit(solution)/shard_map/all_gather | solution.py:102
  7.9 224.3 %reduce-scatter.2.cloned.1.call-start = ((), (), s32[]{:S(2)}) async-start(), calls=%async_computation.2 | async-start | bytes 5242880 | tf_op jit(solution)/shard_map/reduce_scatter | solution.py:105
  8.8 82.3 %collective-permute-start = (bf16[3,2,1024]{2,1,0:T(2,128)(2,1)S(1)}, bf16[3,2,1024]{2,1,0:T(2,128)(2,1)S(1)}, u32[]{:S(2)}, u32[]{:S(2)}) collective-permute-start(bf16[3,2,1024]{2,1,0:T(2,128)(2,1)S(1)} %slice.38), channel_id=1, source_target_pairs={{0,4},{4,8},{8,12},{1,5},{5,9},{9,13},{2,6},{6,10},{10,14},{3,7},{... | collective-permute-start | bytes 36872 | tf_op jit(solution)/shard_map/ppermute | solution.py:13
  15.0 27.0 %copy-start.2 = (f32[1024,8]{1,0:T(8,128)}, f32[1024,8]{1,0:T(8,128)S(1)}, u32[]{:S(2)}) copy-start(f32[1024,8]{1,0:T(8,128)S(1)} %copy.31) | copy-start | bytes 98308
  93.9 1.6 copy-start.1
  102.4 23.6 %copy-start.3 = (f32[1024,8]{1,0:T(8,128)S(1)}, f32[1024,8]{1,0:T(8,128)}, u32[]{:S(2)}) copy-start(f32[1024,8]{1,0:T(8,128)} %copy-done.2) | copy-start | bytes 98308
  126.0 10.4 %copy-start.4 = (f32[4,1024,8]{2,0,1:T(4,128)S(1)}, f32[4,1024,8]{2,0,1:T(4,128)}, u32[]{:S(2)}) copy-start(f32[4,1024,8]{2,0,1:T(4,128)} %copy.38) | copy-start | bytes 393220
  185.7 53.7 %copy-start.6 = (f32[1024]{0:T(1024)S(1)}, f32[1024]{0:T(1024)}, u32[]{:S(2)}) copy-start(f32[1024]{0:T(1024)} %param.17) | copy-start | bytes 12292
  185.7 56.2 %copy-start.7 = (s32[256]{0:T(256)S(1)}, s32[256]{0:T(256)}, u32[]{:S(2)}) copy-start(s32[256]{0:T(256)} %param.20) | copy-start | bytes 3076
  185.8 79.5 %all-gather.7.cloned.1.call-start = ((), (), s32[]{:S(2)}) async-start(), calls=%async_computation.3 | async-start | bytes 2621440 | tf_op jit(solution)/shard_map/all_gather | solution.py:112
  267.2 1.1 copy-start.8
  267.2 3.4 %copy-start.9 = (s32[256]{0:T(256)S(1)}, s32[256]{0:T(256)}, u32[]{:S(2)}) copy-start(s32[256]{0:T(256)} %param.21) | copy-start | bytes 3076
Sparse Core Ops, SparseCore 0:
  9.6 156.0 all-gather.4
  185.9 46.3 reduce-scatter.1
  242.1 23.1 all-gather.6
